TPU v7x, 256 devices: a whole 4x4x8 slice. The times are simulated.
256 devices in a mesh: seg: 4 (over x), sec: 32 (over z, y), rep: 2 (over core).
Axes of the slice: x: 4, y: 4, z: 8, core: 2. Of those that a mesh axis runs over, the one named last changes fastest.
Arguments:
- psi: float32 [4, 64, 256, 256], P('seg', 'sec'), may hold values from -6 to 6
- left_env: bfloat16 [4, 18, 64, 256, 256], P('seg', 'rep', 'sec'), may hold values from -0.375 to 0.375
- right_env: bfloat16 [4, 18, 64, 256, 256], P('seg', 'rep', 'sec'), may hold values from -0.375 to 0.375
- local_block: bfloat16 [4, 64, 256, 256], P('seg', 'sec'), may hold values from -0.375 to 0.375
- kept_left: int32 [4, 64], P('seg', 'sec'), may hold values from 64 to 256
- kept_right: int32 [4, 64], P('seg', 'sec'), may hold values from 64 to 256
- pattern: int32 [4, 18, 64], P('seg', 'rep', 'sec'), may hold values 0 or 1
- term_charge: int32 [18], replicated, may hold values from -2 to 2
Outputs:
- last_vector: float32 [4, 64, 256, 256], P('seg', 'sec')
- coefficients: float32 [4, 8], P('seg')
All inputs are finite; a program needn't handle non-finite values. No bound on the sum of `pattern` on one device may be relied on, other than what follows from the above.
Results may differ from a plain program's by a relative error of at most 0.012.
Values may be sent and summed in bfloat16 or wider, within the bound.
A program may use at most 64 MiB of HBM per device.

v0:
```python
import jax
import jax.numpy as jnp
from jax import lax
from jax.sharding import PartitionSpec as P

ITERS = 4


def extended_2(shard, sides, width):
    for axis, dim in sides:
        size, length = (lax.axis_size(axis), shard.shape[dim])
        up = [(i, (i + 1) % size) for i in range(size - 1)]
        down = [(j, i) for i, j in up]
        last = lax.slice_in_dim(shard, length - width, length, axis=dim)
        first = lax.slice_in_dim(shard, 0, width, axis=dim)
        before = lax.ppermute(last, axis, up)
        after = lax.ppermute(first, axis, down)
        shard = jnp.concatenate([before, shard, after], axis=dim)
    return shard


def from_behind(shard, axis, by):
    length = lax.axis_size(axis)
    return lax.ppermute(shard, axis, [(i, (i + by) % length) for i in range(length)])


def widen(vb):
    return extended_2(vb, (("sec", 0),), 2)


def shifted(extended, charges, first, number):
    index = first + 2 + lax.iota(jnp.int32, number)[None, :] + charges[:, None]
    return extended[index]


def term_action(moved, lefts, rights, pat):
    inner = jnp.einsum("wsij,wsjk->wsik", lefts, moved, preferred_element_type=jnp.float32)
    inner = (inner * pat[:, :, None, None]).astype(jnp.bfloat16)
    return jnp.einsum("wsik,wslk->sil", inner, rights, preferred_element_type=jnp.float32)


def local_action(vb, block):
    first = jnp.einsum("sij,sjk->sik", block, vb, preferred_element_type=jnp.float32)
    return first + jnp.einsum("sij,skj->sik", vb, block, preferred_element_type=jnp.float32)


def lanczos(start, apply_op, mean_of):
    vector = start / jnp.sqrt(mean_of(start * start) + 1e-06)
    prev = jnp.zeros_like(vector)
    beta_prev = jnp.float32(0.0)
    alphas = []
    betas = []
    for step in range(ITERS):
        image = apply_op(vector)
        alpha = mean_of(vector * image)
        image = image - alpha * vector - beta_prev * prev
        beta = jnp.sqrt(mean_of(image * image) + 1e-06)
        prev = vector
        vector = image / beta
        beta_prev = beta
        alphas.append(alpha)
        betas.append(beta)
    return (vector, jnp.stack(alphas + betas))


def on_device(psi, left_env, right_env, local_block, kept_left, kept_right, pattern, term_charge):
    lefts = from_behind(left_env, "seg", 1)[0]
    rights = from_behind(right_env, "seg", -1)[0]
    start = psi[0]
    block = local_block[0]
    width = start.shape[1]
    sectors = start.shape[0]
    terms_here = lefts.shape[0]
    states = lax.iota(jnp.int32, width)
    rows = (states[None, :] < kept_left[0][:, None]).astype(jnp.float32)
    cols = (states[None, :] < kept_right[0][:, None]).astype(jnp.float32)
    projector = rows[:, :, None] * cols[:, None, :]
    count = sectors * lax.axis_size("sec") * width * width
    local_charge = lax.dynamic_slice_in_dim(
        term_charge, lax.axis_index("rep") * terms_here, terms_here, 0
    )
    pat = pattern[0].astype(jnp.float32)

    def apply_whole(vector):
        vb = vector.astype(jnp.bfloat16)
        moved = shifted(widen(vb), local_charge, 0, sectors)
        total = lax.psum(term_action(moved, lefts, rights, pat).astype(jnp.bfloat16), "rep").astype(
            jnp.float32
        )
        return projector * (total + local_action(vb, block))

    def mean_whole(values):
        return lax.psum(jnp.sum(values), "sec") / count

    vector, coeffs = lanczos(projector * start, apply_whole, mean_whole)
    return (vector[None], coeffs[None])


def solution(mesh):
    placed = (
        P("seg", "sec", None, None),
        P("seg", "rep", "sec", None, None),
        P("seg", "rep", "sec", None, None),
        P("seg", "sec", None, None),
        P("seg", "sec"),
        P("seg", "sec"),
        P("seg", "rep", "sec"),
        P(),
    )
    return jax.shard_map(
        on_device,
        mesh=mesh,
        in_specs=placed,
        out_specs=(P("seg", "sec", None, None), P("seg", None)),
        check_vma=False,
    )
```

profile of v0, /device:TPU:8, one launch (start us, length us, event | category | flops | bytes accessed | tf_op | source)
XLA Modules:
  0.0 898.0 jit_solution(11741691733564219125)
XLA Ops:
  7.3 3.4 copy.19
  10.7 2.8 collective-permute-start.3
  14.3 74.4 %psum.91 = f32[]{:T(128)} all-reduce(f32[]{:T(128)} %multiply_reduce_fusion.8), channel_id=1, replica_groups=mesh['seg'=4,'sec'=32,'rep'=2] {'sec'}, use_global_device_ids=true, to_apply=%region_1.0 | all-reduce | flops 1 | bytes 8 | tf_op jit(solution)/shard_map/psum | solution.py:93
  89.6 3.2 collective-permute-start
  92.8 4.6 collective-permute-start.1
  103.7 5.2 fusion.104
  109.2 32.2 %all-reduce.5.cloned.1.call-done = bf16[2,256,256]{2,1,0:T(8,128)(2,1)} async-done(((bf16[2,256,256]{2,1,0:T(8,128)(2,1)}), bf16[2,256,256]{2,1,0:T(8,128)(2,1)}) %all-reduce.5.cloned.1.call-update) | async-done | bytes 262160 | tf_op jit(solution)/shard_map/psum | solution.py:87
  143.4 71.8 %psum.93 = f32[]{:T(128)} all-reduce(f32[]{:T(128)} %get-tuple-element.10), channel_id=1, replica_groups=mesh['seg'=4,'sec'=32,'rep'=2] {'sec'}, use_global_device_ids=true, to_apply=%region_4.0 | all-reduce | flops 1 | bytes 8 | tf_op jit(solution)/shard_map/psum | solution.py:93
  216.7 74.8 %psum.94 = f32[]{:T(128)} all-reduce(f32[]{:T(128)} %multiply_reduce_fusion.6), channel_id=1, replica_groups=mesh['seg'=4,'sec'=32,'rep'=2] {'sec'}, use_global_device_ids=true, to_apply=%region_6.0 | all-reduce | flops 1 | bytes 8 | tf_op jit(solution)/shard_map/psum | solution.py:93
  294.3 3.9 collective-permute-start.5
  305.0 5.2 fusion.113
  310.5 30.3 %all-reduce.7.cloned.1.call-done = bf16[2,256,256]{2,1,0:T(8,128)(2,1)} async-done(((bf16[2,256,256]{2,1,0:T(8,128)(2,1)}), bf16[2,256,256]{2,1,0:T(8,128)(2,1)}) %all-reduce.7.cloned.1.call-update) | async-done | bytes 262160 | tf_op jit(solution)/shard_map/psum | solution.py:87
  342.8 71.8 %psum.96 = f32[]{:T(128)} all-reduce(f32[]{:T(128)} %get-tuple-element.12), channel_id=1, replica_groups=mesh['seg'=4,'sec'=32,'rep'=2] {'sec'}, use_global_device_ids=true, to_apply=%region_9.0 | all-reduce | flops 1 | bytes 8 | tf_op jit(solution)/shard_map/psum | solution.py:93
  416.1 74.8 %psum.97 = f32[]{:T(128)} all-reduce(f32[]{:T(128)} %get-tuple-element.6), channel_id=1, replica_groups=mesh['seg'=4,'sec'=32,'rep'=2] {'sec'}, use_global_device_ids=true, to_apply=%region_11.0 | all-reduce | flops 1 | bytes 8 | tf_op jit(solution)/shard_map/psum | solution.py:93
  493.6 3.9 collective-permute-start.7
  504.3 5.2 fusion.122
  509.8 30.3 %all-reduce.9.cloned.1.call-done = bf16[2,256,256]{2,1,0:T(8,128)(2,1)} async-done(((bf16[2,256,256]{2,1,0:T(8,128)(2,1)}), bf16[2,256,256]{2,1,0:T(8,128)(2,1)}) %all-reduce.9.cloned.1.call-update) | async-done | bytes 262160 | tf_op jit(solution)/shard_map/psum | solution.py:87
  542.1 71.8 %psum.99 = f32[]{:T(128)} all-reduce(f32[]{:T(128)} %get-tuple-element.14), channel_id=1, replica_groups=mesh['seg'=4,'sec'=32,'rep'=2] {'sec'}, use_global_device_ids=true, to_apply=%region_14.0 | all-reduce | flops 1 | bytes 8 | tf_op jit(solution)/shard_map/psum | solution.py:93
  615.3 74.8 %psum.100 = f32[]{:T(128)} all-reduce(f32[]{:T(128)} %get-tuple-element.4), channel_id=1, replica_groups=mesh['seg'=4,'sec'=32,'rep'=2] {'sec'}, use_global_device_ids=true, to_apply=%region_16.0 | all-reduce | flops 1 | bytes 8 | tf_op jit(solution)/shard_map/psum | solution.py:93
  692.8 4.1 collective-permute-start.9
  703.5 5.2 fusion.131
  709.0 30.4 %all-reduce.11.cloned.1.call-done = bf16[2,256,256]{2,1,0:T(8,128)(2,1)} async-done(((bf16[2,256,256]{2,1,0:T(8,128)(2,1)}), bf16[2,256,256]{2,1,0:T(8,128)(2,1)}) %all-reduce.11.cloned.1.call-update) | async-done | bytes 262160 | tf_op jit(solution)/shard_map/psum | solution.py:87
  741.3 71.8 %psum.102 = f32[]{:T(128)} all-reduce(f32[]{:T(128)} %get-tuple-element.16), channel_id=1, replica_groups=mesh['seg'=4,'sec'=32,'rep'=2] {'sec'}, use_global_device_ids=true, to_apply=%region_19.0 | all-reduce | flops 1 | bytes 8 | tf_op jit(solution)/shard_map/psum | solution.py:93
  814.6 74.8 %psum.103 = f32[]{:T(128)} all-reduce(f32[]{:T(128)} %get-tuple-element.2), channel_id=1, replica_groups=mesh['seg'=4,'sec'=32,'rep'=2] {'sec'}, use_global_device_ids=true, to_apply=%region_21.0 | all-reduce | flops 1 | bytes 8 | tf_op jit(solution)/shard_map/psum | solution.py:93
  (76 shorter events, 47.4 us)
Async XLA Ops:
  7.2 101.8 %copy-start = (bf16[1,2,256,256]{3,2,1,0:T(8,128)(2,1)S(1)}, bf16[1,2,256,256]{3,2,1,0:T(8,128)(2,1)}, u32[]{:S(2)}) copy-start(bf16[1,2,256,256]{3,2,1,0:T(8,128)(2,1)} %param.11) | copy-start | bytes 786436
  7.2 6.3 copy-start.8
  7.2 6.2 copy-start.7
  7.2 6.3 copy-start.1
  7.2 90.2 %copy-start.9 = (s32[18]{0:T(128)S(1)}, s32[18]{0:T(128)}, u32[]{:S(2)}) copy-start(s32[18]{0:T(128)} %param.15) | copy-start | bytes 220
  7.2 90.4 %copy-start.6 = (s32[1,9,2]{1,2,0:T(2,128)S(1)}, s32[1,9,2]{1,2,0:T(2,128)}, u32[]{:S(2)}) copy-start(s32[1,9,2]{1,2,0:T(2,128)} %param.14) | copy-start | bytes 220
  7.2 134.2 %all-reduce.5.cloned.1.call-start = ((), (), s32[]{:S(2)}) async-start(), calls=%async_computation | async-start | bytes 524288 | tf_op jit(solution)/shard_map/psum | solution.py:87
  10.7 93.0 %collective-permute-start.3 = (bf16[1,9,2,256,256]{4,3,1,2,0:T(8,128)(2,1)}, bf16[1,9,2,256,256]{4,3,1,2,0:T(8,128)(2,1)}, u32[]{:S(2)}, u32[]{:S(2)}) collective-permute-start(bf16[1,9,2,256,256]{4,3,1,2,0:T(8,128)(2,1)} %copy.19), channel_id=1, source_target_pairs={{0,192},{64,0},{128,64},{192,128},{1,193},{65,1},{129,65},{193,129... | collective-permute-start | bytes 7077896 | tf_op jit(solution)/shard_map/ppermute | solution.py:24
  13.4 90.3 %collective-permute-start.2 = (bf16[1,9,2,256,256]{4,3,2,1,0:T(8,128)(2,1)}, bf16[1,9,2,256,256]{4,3,2,1,0:T(8,128)(2,1)}, u32[]{:S(2)}, u32[]{:S(2)}) collective-permute-start(bf16[1,9,2,256,256]{4,3,2,1,0:T(8,128)(2,1)} %param.9), channel_id=1, source_target_pairs={{0,64},{64,128},{128,192},{192,0},{1,65},{65,129},{129,193},{193,1... | collective-permute-start | bytes 7077896 | tf_op jit(solution)/shard_map/ppermute | solution.py:24
  89.6 10.2 %collective-permute-start = (bf16[2,256,256]{2,1,0:T(8,128)(2,1)S(1)}, bf16[2,256,256]{2,1,0:T(8,128)(2,1)S(1)}, u32[]{:S(2)}, u32[]{:S(2)}) collective-permute-start(bf16[2,256,256]{2,1,0:T(8,128)(2,1)S(1)} %fusion.155), channel_id=1, source_target_pairs={{0,2},{2,4},{4,6},{6,8},{8,10},{10,12},{12,14},{14,16},{16,18},{18... | collective-permute-start | bytes 786440 | tf_op jit(solution)/shard_map/ppermute | solution.py:16
  92.8 8.5 collective-permute-start.1
  108.9 231.9 %all-reduce.7.cloned.1.call-start = ((), (), s32[]{:S(2)}) async-start(), calls=%async_computation.1 | async-start | bytes 524288 | tf_op jit(solution)/shard_map/psum | solution.py:87
  141.4 74.3 %copy-start.2 = (bf16[2,256,256]{2,1,0:T(8,128)(2,1)S(1)}, bf16[2,256,256]{2,1,0:T(8,128)(2,1)}, u32[]{:S(2)}) copy-start(bf16[2,256,256]{2,1,0:T(8,128)(2,1)} %all-reduce.5.cloned.1.call-done) | copy-start | bytes 786436
  292.4 8.3 collective-permute-start.4
  294.3 8.3 collective-permute-start.5
  310.2 229.9 %all-reduce.9.cloned.1.call-start = ((), (), s32[]{:S(2)}) async-start(), calls=%async_computation.2 | async-start | bytes 524288 | tf_op jit(solution)/shard_map/psum | solution.py:87
  340.9 74.3 %copy-start.3 = (bf16[2,256,256]{2,1,0:T(8,128)(2,1)S(1)}, bf16[2,256,256]{2,1,0:T(8,128)(2,1)}, u32[]{:S(2)}) copy-start(bf16[2,256,256]{2,1,0:T(8,128)(2,1)} %all-reduce.7.cloned.1.call-done) | copy-start | bytes 786436
  491.7 8.3 collective-permute-start.6
  493.6 8.3 collective-permute-start.7
  509.5 229.9 %all-reduce.11.cloned.1.call-start = ((), (), s32[]{:S(2)}) async-start(), calls=%async_computation.3 | async-start | bytes 524288 | tf_op jit(solution)/shard_map/psum | solution.py:87
  540.1 74.3 %copy-start.4 = (bf16[2,256,256]{2,1,0:T(8,128)(2,1)S(1)}, bf16[2,256,256]{2,1,0:T(8,128)(2,1)}, u32[]{:S(2)}) copy-start(bf16[2,256,256]{2,1,0:T(8,128)(2,1)} %all-reduce.9.cloned.1.call-done) | copy-start | bytes 786436
  690.9 8.3 collective-permute-start.8
  692.8 8.3 collective-permute-start.9
  739.4 74.3 %copy-start.5 = (bf16[2,256,256]{2,1,0:T(8,128)(2,1)S(1)}, bf16[2,256,256]{2,1,0:T(8,128)(2,1)}, u32[]{:S(2)}) copy-start(bf16[2,256,256]{2,1,0:T(8,128)(2,1)} %all-reduce.11.cloned.1.call-done) | copy-start | bytes 786436
Sparse Core Ops, SparseCore 0:
  109.0 32.3 all-reduce.4
  310.3 30.4 all-reduce.6
  509.6 30.4 all-reduce.8
  708.8 30.4 all-reduce.10
where the time goes:
time: 899 us; the launch traced here: 898 us
  blocking collectives  661 us (74%)
  waiting for transfers between devices  140 us (16%)
  matrix products  29.6 us (3%)
  starting transfers between devices  28.5 us (3%)
  between operations  20.1 us (2%)
  local copies, waits for them, and re-layouts  13.5 us (2%)
    psum x9, blocking collectives, mean_whole(): return lax.psum(jnp.sum(values), 'sec') / count  661 us
    psum x4, waiting for transfers between devices, apply_whole(): lax.psum(term_action(moved, lefts, rights, pat).astype(jnp.bfloat16), 'rep')  123 us
    dot_general x4, matrix products, term_action(): jnp.einsum('wsik,wslk->sil', inner, rights, preferred_element_type=jnp.fl...  20.8 us
  transfers between devices with their start and end apart: 14, of which 12 were waited for; matrix products, arithmetic and copies ran while one was open for 1% of the time, Pallas kernels for 0%

commit v1 on v0

--- a/solution.py
+++ b/solution.py
@@ -84,9 +84,10 @@
     def apply_whole(vector):
         vb = vector.astype(jnp.bfloat16)
         moved = shifted(widen(vb), local_charge, 0, sectors)
-        total = lax.psum(term_action(moved, lefts, rights, pat).astype(jnp.bfloat16), "rep").astype(
-            jnp.float32
-        )
+        total = jnp.sum(
+            lax.all_gather(term_action(moved, lefts, rights, pat).astype(jnp.bfloat16), "rep"),
+            axis=0,
+        ).astype(jnp.float32)
         return projector * (total + local_action(vb, block))
 
     def mean_whole(values):

time: 899 us -> 761 us (0.85)
  waiting for transfers between devices: 140 us -> 18.1 us
  between operations: 20.1 us -> 7.04 us
    psum x4 -> x0, waiting for transfers between devices: 123 us -> none  [apply_whole(): lax.psum(term_action(moved, lefts, rights, pat).astype(jnp.bfloat16), 'rep')]
    psum x9, blocking collectives: 661 us -> 645 us  [mean_whole(): return lax.psum(jnp.sum(values), 'sec') / count]
  transfers between devices with their start and end apart: 14 -> 10, of which waited for: 12 -> 8; matrix products, arithmetic and copies ran while one was open for 1% -> 1% of each run, Pallas kernels for 0% -> 0%
where the time goes in v1:
time: 761 us; the launch traced here: 753 us
  blocking collectives  653 us (86%)
  starting transfers between devices  28.6 us (4%)
  matrix products  22.9 us (3%)
  waiting for transfers between devices  18.1 us (2%)
  local copies, waits for them, and re-layouts  16.8 us (2%)
    psum x9, blocking collectives, mean_whole(): return lax.psum(jnp.sum(values), 'sec') / count  645 us
    dot_general x4, matrix products, term_action(): jnp.einsum('wsik,wslk->sil', inner, rights, preferred_element_type=jnp.fl...  18.2 us
  transfers between devices with their start and end apart: 10, of which 8 were waited for; matrix products, arithmetic and copies ran while one was open for 1% of the time, Pallas kernels for 0%

profile of v1, /device:TPU:8, one launch (start us, length us, event | category | flops | bytes accessed | tf_op | source)
XLA Modules:
  0.0 752.6 jit_solution(14964991319230918834)
XLA Ops:
  0.7 3.5 copy.35
  4.1 2.8 collective-permute-start.3
  9.6 74.5 %psum.63 = f32[]{:T(128)} all-reduce(f32[]{:T(128)} %multiply_reduce_fusion.8), channel_id=1, replica_groups=mesh['seg'=4,'sec'=32,'rep'=2] {'sec'}, use_global_device_ids=true, to_apply=%region_1.0 | all-reduce | flops 1 | bytes 8 | tf_op jit(solution)/shard_map/psum | solution.py:94
  85.0 6.4 collective-permute-start.1
  95.3 4.4 collective-permute-done
  99.7 2.3 gather_fusion
  102.0 4.6 fusion.108
  110.0 69.8 %psum.64 = f32[]{:T(128)} all-reduce(f32[]{:T(128)} %get-tuple-element.16), channel_id=1, replica_groups=mesh['seg'=4,'sec'=32,'rep'=2] {'sec'}, use_global_device_ids=true, to_apply=%region_4.0 | all-reduce | flops 1 | bytes 8 | tf_op jit(solution)/shard_map/psum | solution.py:94
  181.3 72.7 %psum.65 = f32[]{:T(128)} all-reduce(f32[]{:T(128)} %multiply_reduce_fusion.6), channel_id=1, replica_groups=mesh['seg'=4,'sec'=32,'rep'=2] {'sec'}, use_global_device_ids=true, to_apply=%region_6.0 | all-reduce | flops 1 | bytes 8 | tf_op jit(solution)/shard_map/psum | solution.py:94
  256.9 3.9 collective-permute-start.4
  265.2 2.3 gather_fusion.1
  267.5 4.6 fusion.117
  275.6 69.8 %psum.66 = f32[]{:T(128)} all-reduce(f32[]{:T(128)} %get-tuple-element.18), channel_id=1, replica_groups=mesh['seg'=4,'sec'=32,'rep'=2] {'sec'}, use_global_device_ids=true, to_apply=%region_9.0 | all-reduce | flops 1 | bytes 8 | tf_op jit(solution)/shard_map/psum | solution.py:94
  346.9 72.7 %psum.67 = f32[]{:T(128)} all-reduce(f32[]{:T(128)} %get-tuple-element.12), channel_id=1, replica_groups=mesh['seg'=4,'sec'=32,'rep'=2] {'sec'}, use_global_device_ids=true, to_apply=%region_11.0 | all-reduce | flops 1 | bytes 8 | tf_op jit(solution)/shard_map/psum | solution.py:94
  422.2 3.9 collective-permute-start.6
  430.6 2.3 gather_fusion.2
  432.9 4.6 fusion.126
  440.9 70.0 %psum.68 = f32[]{:T(128)} all-reduce(f32[]{:T(128)} %get-tuple-element.20), channel_id=1, replica_groups=mesh['seg'=4,'sec'=32,'rep'=2] {'sec'}, use_global_device_ids=true, to_apply=%region_14.0 | all-reduce | flops 1 | bytes 8 | tf_op jit(solution)/shard_map/psum | solution.py:94
  512.3 72.7 %psum.69 = f32[]{:T(128)} all-reduce(f32[]{:T(128)} %get-tuple-element.10), channel_id=1, replica_groups=mesh['seg'=4,'sec'=32,'rep'=2] {'sec'}, use_global_device_ids=true, to_apply=%region_16.0 | all-reduce | flops 1 | bytes 8 | tf_op jit(solution)/shard_map/psum | solution.py:94
  587.7 3.9 collective-permute-start.8
  596.0 2.3 gather_fusion.3
  598.4 4.6 fusion.135
  606.4 69.8 %psum.70 = f32[]{:T(128)} all-reduce(f32[]{:T(128)} %get-tuple-element.22), channel_id=1, replica_groups=mesh['seg'=4,'sec'=32,'rep'=2] {'sec'}, use_global_device_ids=true, to_apply=%region_19.0 | all-reduce | flops 1 | bytes 8 | tf_op jit(solution)/shard_map/psum | solution.py:94
  677.6 72.7 %psum.71 = f32[]{:T(128)} all-reduce(f32[]{:T(128)} %get-tuple-element.8), channel_id=1, replica_groups=mesh['seg'=4,'sec'=32,'rep'=2] {'sec'}, use_global_device_ids=true, to_apply=%region_21.0 | all-reduce | flops 1 | bytes 8 | tf_op jit(solution)/shard_map/psum | solution.py:94
  (73 shorter events, 44.7 us)
Async XLA Ops:
  0.6 93.0 %copy-start = (bf16[1,2,256,256]{3,2,1,0:T(8,128)(2,1)S(1)}, bf16[1,2,256,256]{3,2,1,0:T(8,128)(2,1)}, u32[]{:S(2)}) copy-start(bf16[1,2,256,256]{3,2,1,0:T(8,128)(2,1)} %param.11) | copy-start | bytes 786436
  0.6 6.2 copy-start.1
  4.1 4.4 copy-start.2
  4.1 4.6 copy-start.4
  4.1 4.6 copy-start.5
  4.1 97.9 %collective-permute-start.3 = (bf16[1,9,2,256,256]{4,3,1,2,0:T(8,128)(2,1)}, bf16[1,9,2,256,256]{4,3,1,2,0:T(8,128)(2,1)}, u32[]{:S(2)}, u32[]{:S(2)}) collective-permute-start(bf16[1,9,2,256,256]{4,3,1,2,0:T(8,128)(2,1)} %copy.35), channel_id=1, source_target_pairs={{0,192},{64,0},{128,64},{192,128},{1,193},{65,1},{129,65},{193,129... | collective-permute-start | bytes 7077896 | tf_op jit(solution)/shard_map/ppermute | solution.py:24
  8.5 84.8 %copy-start.6 = (s32[18]{0:T(128)S(1)}, s32[18]{0:T(128)}, u32[]{:S(2)}) copy-start(s32[18]{0:T(128)} %param.15) | copy-start | bytes 220
  8.5 85.1 %copy-start.3 = (s32[1,9,2]{1,2,0:T(2,128)S(1)}, s32[1,9,2]{1,2,0:T(2,128)}, u32[]{:S(2)}) copy-start(s32[1,9,2]{1,2,0:T(2,128)} %param.14) | copy-start | bytes 220
  8.5 93.5 %collective-permute-start.2 = (bf16[1,9,2,256,256]{4,3,1,2,0:T(8,128)(2,1)}, bf16[1,9,2,256,256]{4,3,1,2,0:T(8,128)(2,1)}, u32[]{:S(2)}, u32[]{:S(2)}) collective-permute-start(bf16[1,9,2,256,256]{4,3,1,2,0:T(8,128)(2,1)} %copy.33), channel_id=1, source_target_pairs={{0,64},{64,128},{128,192},{192,0},{1,65},{65,129},{129,193},{193,1... | collective-permute-start | bytes 7077896 | tf_op jit(solution)/shard_map/ppermute | solution.py:24
  85.0 10.3 %collective-permute-start.1 = (bf16[2,256,256]{1,2,0:T(8,128)(2,1)S(1)}, bf16[2,256,256]{1,2,0:T(8,128)(2,1)S(1)}, u32[]{:S(2)}, u32[]{:S(2)}) collective-permute-start(bf16[2,256,256]{1,2,0:T(8,128)(2,1)S(1)} %fusion.159), channel_id=1, source_target_pairs={{2,0},{4,2},{6,4},{8,6},{10,8},{12,10},{14,12},{16,14},{18,16},{20... | collective-permute-start | bytes 786440 | tf_op jit(solution)/shard_map/ppermute | solution.py:17
  91.4 8.3 %collective-permute-start = (bf16[2,256,256]{1,2,0:T(8,128)(2,1)S(1)}, bf16[2,256,256]{1,2,0:T(8,128)(2,1)S(1)}, u32[]{:S(2)}, u32[]{:S(2)}) collective-permute-start(bf16[2,256,256]{1,2,0:T(8,128)(2,1)S(1)} %fusion.159), channel_id=1, source_target_pairs={{0,2},{2,4},{4,6},{6,8},{8,10},{10,12},{12,14},{14,16},{16,18},{18... | collective-permute-start | bytes 786440 | tf_op jit(solution)/shard_map/ppermute | solution.py:16
  254.9 8.3 %collective-permute-start.5 = (bf16[2,256,256]{1,2,0:T(8,128)(2,1)S(1)}, bf16[2,256,256]{1,2,0:T(8,128)(2,1)S(1)}, u32[]{:S(2)}, u32[]{:S(2)}) collective-permute-start(bf16[2,256,256]{1,2,0:T(8,128)(2,1)S(1)} %get-tuple-element.14), channel_id=1, source_target_pairs={{2,0},{4,2},{6,4},{8,6},{10,8},{12,10},{14,12},{16,14},{18,16},{20... | collective-permute-start | bytes 786440 | tf_op jit(solution)/shard_map/ppermute | solution.py:17
  256.9 8.3 %collective-permute-start.4 = (bf16[2,256,256]{1,2,0:T(8,128)(2,1)S(1)}, bf16[2,256,256]{1,2,0:T(8,128)(2,1)S(1)}, u32[]{:S(2)}, u32[]{:S(2)}) collective-permute-start(bf16[2,256,256]{1,2,0:T(8,128)(2,1)S(1)} %get-tuple-element.14), channel_id=1, source_target_pairs={{0,2},{2,4},{4,6},{6,8},{8,10},{10,12},{12,14},{14,16},{16,18},{18... | collective-permute-start | bytes 786440 | tf_op jit(solution)/shard_map/ppermute | solution.py:16
  420.3 8.3 %collective-permute-start.7 = (bf16[2,256,256]{1,2,0:T(8,128)(2,1)S(1)}, bf16[2,256,256]{1,2,0:T(8,128)(2,1)S(1)}, u32[]{:S(2)}, u32[]{:S(2)}) collective-permute-start(bf16[2,256,256]{1,2,0:T(8,128)(2,1)S(1)} %fusion.158), channel_id=1, source_target_pairs={{2,0},{4,2},{6,4},{8,6},{10,8},{12,10},{14,12},{16,14},{18,16},{20... | collective-permute-start | bytes 786440 | tf_op jit(solution)/shard_map/ppermute | solution.py:17
  422.2 8.3 %collective-permute-start.6 = (bf16[2,256,256]{1,2,0:T(8,128)(2,1)S(1)}, bf16[2,256,256]{1,2,0:T(8,128)(2,1)S(1)}, u32[]{:S(2)}, u32[]{:S(2)}) collective-permute-start(bf16[2,256,256]{1,2,0:T(8,128)(2,1)S(1)} %fusion.158), channel_id=1, source_target_pairs={{0,2},{2,4},{4,6},{6,8},{8,10},{10,12},{12,14},{14,16},{16,18},{18... | collective-permute-start | bytes 786440 | tf_op jit(solution)/shard_map/ppermute | solution.py:16
  585.7 8.3 %collective-permute-start.9 = (bf16[2,256,256]{1,2,0:T(8,128)(2,1)S(1)}, bf16[2,256,256]{1,2,0:T(8,128)(2,1)S(1)}, u32[]{:S(2)}, u32[]{:S(2)}) collective-permute-start(bf16[2,256,256]{1,2,0:T(8,128)(2,1)S(1)} %fusion.157), channel_id=1, source_target_pairs={{2,0},{4,2},{6,4},{8,6},{10,8},{12,10},{14,12},{16,14},{18,16},{20... | collective-permute-start | bytes 786440 | tf_op jit(solution)/shard_map/ppermute | solution.py:17
  587.7 8.3 %collective-permute-start.8 = (bf16[2,256,256]{1,2,0:T(8,128)(2,1)S(1)}, bf16[2,256,256]{1,2,0:T(8,128)(2,1)S(1)}, u32[]{:S(2)}, u32[]{:S(2)}) collective-permute-start(bf16[2,256,256]{1,2,0:T(8,128)(2,1)S(1)} %fusion.157), channel_id=1, source_target_pairs={{0,2},{2,4},{4,6},{6,8},{8,10},{10,12},{12,14},{14,16},{16,18},{18... | collective-permute-start | bytes 786440 | tf_op jit(solution)/shard_map/ppermute | solution.py:16
